TPU v7x, 256 devices: a whole 4x4x8 slice. The times are simulated.
256 devices in a mesh: row: 16 (over z, core), col: 8 (over x_hi, y), feat: 2 (over x_lo).
Axes of the slice: x: 4 (x_hi: 2, x_lo: 2; x = x_hi * 2 + x_lo), y: 4, z: 8, core: 2. Of those that a mesh axis runs over, the one named last changes fastest.
Arguments:
- features: bfloat16 [65536, 256], P(('col', 'row'), 'feat'), may hold values from -6 to 6
- tile_rows: int32 [16, 8, 256], P('row', 'col'), may hold values from 0 to 31, as said below
- tile_cols: int32 [16, 8, 256], P('row', 'col'), may hold values from 0 to 63
- tile_count: int32 [16, 8], P('row', 'col'), may hold values from 64 to 256, as said below
- tile_values: bfloat16 [16, 8, 256, 128, 128], P('row', 'col'), may hold values from -0.21875 to 0.21875
- weights: bfloat16 [256, 256], replicated, may hold values from -0.375 to 0.375
- cotangent: bfloat16 [65536, 256], P(('row', 'col'), 'feat'), may hold values from -6 to 6
Outputs:
- activated: bfloat16 [65536, 256], P(('row', 'col'), 'feat')
- feature_grad: bfloat16 [65536, 256], P(('col', 'row'), 'feat')
- weight_grad: float32 [256, 256], P('feat')
Inputs may be any that keep to these rules, and one draw needn't show every extreme that they name: `tile_rows`: block rows of a cell, unevenly loaded. `tile_count`: some cell has all 256 slots live.
All inputs are finite; a program needn't handle non-finite values.
Results may differ from a plain program's by a relative error of at most 0.027.
Values may be sent and summed in bfloat16 or wider, within the bound.
A program may use at most 128 MiB of HBM per device.

v0:
```python
import jax
import jax.numpy as jnp
from jax import lax
from jax.sharding import PartitionSpec as P


def shards(features, tile_rows, tile_cols, tile_count, tile_values, weights, cotangent):
    width = tile_values.shape[-1]
    slots = tile_values.shape[2]
    local_tiles = tile_values[0, 0]
    block_rows = tile_rows[0, 0]
    block_cols = tile_cols[0, 0]
    live_mask = (jnp.arange(slots) < tile_count[0, 0]).astype(jnp.float32)
    n_rowdev = lax.axis_size("row")
    n_coldev = lax.axis_size("col")
    local_blocks = features.shape[0] // width
    feat_half = features.shape[1]
    feat_index = lax.axis_index("feat")
    row_blocks = local_blocks * n_coldev
    col_blocks = local_blocks * n_rowdev
    node_total = features.shape[0] * n_rowdev * n_coldev
    panel = lax.all_gather(features, "row", axis=0, tiled=True)
    gathered = panel.reshape(col_blocks, width, feat_half)[block_cols]
    products = jnp.einsum("tij,tjf->tif", local_tiles, gathered, preferred_element_type=jnp.float32)
    products = products * live_mask[:, None, None]
    partial_value = (
        jnp.zeros((row_blocks, width, feat_half), jnp.float32).at[block_rows].add(products)
    )
    summed = lax.psum_scatter(
        partial_value.reshape(row_blocks * width, feat_half).astype(jnp.bfloat16),
        "col",
        scatter_dimension=0,
        tiled=True,
    )
    weight_rows = lax.dynamic_slice_in_dim(weights, feat_index * feat_half, feat_half, 0)
    mix_term = jnp.dot(summed, weight_rows, preferred_element_type=jnp.float32)
    hidden = lax.psum_scatter(
        mix_term.astype(jnp.bfloat16), "feat", scatter_dimension=1, tiled=True
    ).astype(jnp.float32)
    negative = jnp.minimum(hidden, 0.0)
    activated = jnp.where(hidden > 0, hidden, jnp.expm1(negative)).astype(jnp.bfloat16)
    slope_factor = jnp.where(hidden > 0, 1.0, jnp.exp(negative))
    grad_out = (cotangent.astype(jnp.float32) * slope_factor).astype(jnp.bfloat16)
    grad_whole = lax.all_gather(grad_out, "feat", axis=1, tiled=True)
    weight_term = lax.dot_general(
        summed, grad_whole, (((0,), (0,)), ((), ())), preferred_element_type=jnp.float32
    )
    weight_grad = lax.psum(weight_term, ("row", "col")) * node_total ** (-0.5)
    spread = lax.dot_general(
        grad_whole, weight_rows, (((1,), (1,)), ((), ())), preferred_element_type=jnp.float32
    ).astype(jnp.bfloat16)
    spread_panel = lax.all_gather(spread, "col", axis=0, tiled=True)
    spread_blocks = spread_panel.reshape(row_blocks, width, feat_half)[block_rows]
    back_products = jnp.einsum(
        "tji,tjf->tif", local_tiles, spread_blocks, preferred_element_type=jnp.float32
    )
    back_products = back_products * live_mask[:, None, None]
    back_partial = (
        jnp.zeros((col_blocks, width, feat_half), jnp.float32).at[block_cols].add(back_products)
    )
    back_summed = lax.psum_scatter(
        back_partial.reshape(col_blocks * width, feat_half).astype(jnp.bfloat16),
        "row",
        scatter_dimension=0,
        tiled=True,
    )
    return (activated, back_summed, weight_grad)


def solution(mesh):
    return jax.shard_map(
        shards,
        mesh=mesh,
        in_specs=(
            P(("col", "row"), "feat"),
            P("row", "col", None),
            P("row", "col", None),
            P("row", "col"),
            P("row", "col", None, None, None),
            P(),
            P(("row", "col"), "feat"),
        ),
        out_specs=(P(("row", "col"), "feat"), P(("col", "row"), "feat"), P("feat", None)),
        check_vma=False,
    )
```

profile of v0, /device:TPU:2, one launch (start us, length us, event | category | flops | bytes accessed | tf_op | source)
XLA Modules:
  0.0 1467.3 jit_solution(11761849151452895008)
XLA Ops:
  7.2 0.7 all-gather.3.cloned.1.call-update
  8.6 0.7 compare_select_fusion
  9.3 0.7 compare_select_fusion.1
  10.0 42.6 %all-gather.3.cloned.1.call-done = bf16[8192,128]{1,0:T(8,128)(2,1)} async-done(((bf16[512,128]{1,0:T(8,128)(2,1)}), bf16[8192,128]{1,0:T(8,128)(2,1)}) %all-gather.3.cloned.1.call-update) | async-done | bytes 2097168 | tf_op jit(solution)/shard_map/all_gather | solution.py:22
  52.6 10.2 gather_fusion
  62.8 13.0 multiply_bitcast_fusion.1
  75.8 17.5 %copy.17 = f32[256,128,128]{2,1,0:T(8,128)} copy(f32[256,128,128]{1,2,0:T(8,128)} %multiply_bitcast_fusion.1) | data formatting | bytes 33554432 | tf_op jit(solution)/shard_map/mul | solution.py:25
  93.2 0.2 broadcast_in_dim.8
  93.5 33.2 %scatter_fusion = f32[32,128,128]{2,1,0:T(8,128)S(1)} fusion(f32[32,128,128]{2,1,0:T(8,128)S(1)} %broadcast_in_dim.8, s32[256]{0:T(256)S(1)} %bitcast.37, f32[256,128,128]{2,1,0:T(8,128)} %copy.17), kind=kCustom, calls=%fused_computation.2 | custom fusion | flops 4194304 | bytes 50332672 | tf_op jit(solution)/shard_map/scatter-add | solution.py:27
  126.6 1.1 convert_element_type.38
  127.8 0.0 reduce-scatter.10.cloned.1.call-start
  127.9 74.5 %reduce-scatter.6.cloned.1.call-done = bf16[512,128]{1,0:T(8,128)(2,1)} async-done(((bf16[4096,128]{1,0:T(8,128)(2,1)}), bf16[512,128]{1,0:T(8,128)(2,1)}) %reduce-scatter.6.cloned.1.call-update) | async-done | bytes 131088 | tf_op jit(solution)/shard_map/reduce_scatter | solution.py:29
  202.3 1.1 convolution_convert_fusion
  203.5 0.8 copy.22
  204.3 0.0 all-gather.5.cloned.1.call-start
  204.4 16.0 %reduce-scatter.10.cloned.1.call-done = bf16[128,512]{1,0:T(8,128)(2,1)} async-done(((bf16[256,512]{1,0:T(8,128)(2,1)}), bf16[128,512]{1,0:T(8,128)(2,1)}) %reduce-scatter.10.cloned.1.call-update) | async-done | bytes 131088
  220.4 1.0 copy.23
  221.4 0.8 fusion.6
  222.2 5.9 all_gather.10
  228.1 0.9 convolution_convert_fusion.1
  229.1 1.8 fusion.12
  230.9 0.2 reduce-scatter.8.cloned.1.call-start
  231.2 50.7 %all-gather.5.cloned.1.call-done = bf16[4096,128]{1,0:T(8,128)(2,1)} async-done(((bf16[512,128]{1,0:T(8,128)(2,1)}), bf16[4096,128]{1,0:T(8,128)(2,1)}) %all-gather.5.cloned.1.call-update) | async-done | bytes 1048592 | tf_op jit(solution)/shard_map/all_gather | solution.py:52
  281.9 9.8 gather_fusion.1
  291.7 15.4 %multiply_bitcast_fusion = f32[256,128,128]{1,2,0:T(8,128)} fusion(bf16[256,128,128]{2,1,0:T(8,128)(2,1)} %gather_fusion.1, bf16[1,1,256,128,128]{4,3,2,1,0:T(8,128)(2,1)} %param.11, f32[256]{0:T(256)S(1)} %compare_convert_fusion), kind=kOutput, calls=%fused_computation.4 | convolution fusion | flops 1077936128 | bytes 33555456 | tf_op jit(solution)/shard_map/tji,tjf->tif/dot_general | solution.py:54
  307.1 17.4 %copy.19 = f32[256,128,128]{2,1,0:T(8,128)} copy(f32[256,128,128]{1,2,0:T(8,128)} %multiply_bitcast_fusion) | data formatting | bytes 33554432 | tf_op jit(solution)/shard_map/mul | solution.py:57
  324.5 2.4 broadcast_in_dim.9
  327.0 51.9 %scatter_fusion.1 = f32[64,128,128]{2,1,0:T(8,128)} fusion(f32[64,128,128]{2,1,0:T(8,128)} %broadcast_in_dim.9, s32[256]{0:T(256)S(1)} %bitcast.36, f32[256,128,128]{2,1,0:T(8,128)} %copy.19), kind=kCustom, calls=%fused_computation.3 | custom fusion | flops 4194304 | bytes 50332672 | tf_op jit(solution)/shard_map/scatter-add | solution.py:59
  378.8 3.9 convert_element_type.46
  382.8 1018.1 %all-reduce.2.cloned.1.call-done = f32[128,256]{1,0:T(8,128)} async-done(((f32[128,256]{1,0:T(8,128)}), f32[128,256]{1,0:T(8,128)}) %all-reduce.2.cloned.1.call-update) | async-done | bytes 131088 | tf_op jit(solution)/shard_map/psum | solution.py:48
  1400.8 1.6 broadcast_multiply_fusion
  1402.4 58.0 %reduce-scatter.8.cloned.1.call-done = bf16[512,128]{1,0:T(8,128)(2,1)} async-done(((bf16[8192,128]{1,0:T(8,128)(2,1)}), bf16[512,128]{1,0:T(8,128)(2,1)}) %reduce-scatter.8.cloned.1.call-update) | async-done | bytes 131088 | tf_op jit(solution)/shard_map/reduce_scatter | solution.py:61
  (17 shorter events, 0.2 us)
Async XLA Ops:
  7.2 195.2 %copy-start = (bf16[256,256]{1,0:T(8,128)(2,1)S(1)}, bf16[256,256]{1,0:T(8,128)(2,1)}, u32[]{:S(2)}) copy-start(bf16[256,256]{1,0:T(8,128)(2,1)} %param.12) | copy-start | bytes 393220
  7.2 45.4 %all-gather.3.cloned.1.call-start = ((), (), s32[]{:S(2)}) async-start(), calls=%async_computation.3 | async-start | bytes 2228224 | tf_op jit(solution)/shard_map/all_gather | solution.py:22
  7.9 194.4 %reduce-scatter.6.cloned.1.call-start = ((), (), s32[]{:S(2)}) async-start(), calls=%async_computation.4 | async-start | bytes 1179648 | tf_op jit(solution)/shard_map/reduce_scatter | solution.py:29
  93.4 128.0 %copy-start.2 = (bf16[512,128]{1,0:T(8,128)(2,1)S(1)}, bf16[512,128]{1,0:T(8,128)(2,1)}, u32[]{:S(2)}) copy-start(bf16[512,128]{1,0:T(8,128)(2,1)} %param.13) | copy-start | bytes 393220
  127.8 92.6 %reduce-scatter.10.cloned.1.call-start = ((), (), s32[]{:S(2)}) async-start(), calls=%async_computation.8 | async-start | bytes 393216
  204.3 77.5 %all-gather.5.cloned.1.call-start = ((), (), s32[]{:S(2)}) async-start(), calls=%async_computation.5 | async-start | bytes 1179648 | tf_op jit(solution)/shard_map/all_gather | solution.py:52
  229.0 1171.8 %all-reduce.2.cloned.1.call-start = ((), (), s32[]{:S(2)}) async-start(), calls=%async_computation.7 | async-start | bytes 262144 | tf_op jit(solution)/shard_map/psum | solution.py:48
  230.9 1229.5 %reduce-scatter.8.cloned.1.call-start = ((), (), s32[]{:S(2)}) async-start(), calls=%async_computation.6 | async-start | bytes 2228224 | tf_op jit(solution)/shard_map/reduce_scatter | solution.py:61
  327.0 1133.5 %copy-start.1 = (bf16[256,256]{1,0:T(8,128)(2,1)S(1)}, bf16[256,256]{1,0:T(8,128)(2,1)}, u32[]{:S(2)}) copy-start(bf16[256,256]{1,0:T(8,128)(2,1)} %param.12) | copy-start | bytes 393220
Sparse Core Ops, SparseCore 0:
  9.8 42.6 all-gather.2
  127.9 74.3 reduce-scatter.5
  205.0 15.3 reduce-scatter.9
  229.2 52.6 all-gather.4
  284.9 1115.9 all-reduce.1
  1404.0 56.4 reduce-scatter.7
where the time goes:
time: 1470 us
  waiting for transfers between devices  1260 us (86%)
  other arithmetic  93.8 us (6%)
  local copies, waits for them, and re-layouts  59.5 us (4%)
  matrix products  32.2 us (2%)
  between operations  14.8 us (1%)
    psum x1, waiting for transfers between devices, shards(): weight_grad = lax.psum(weight_term, ('row', 'col')) * node_total ** (-0.5)  1020 us
    reduce_scatter x1, waiting for transfers between devices, shards(): lax.psum_scatter(partial_value.reshape(row_blocks * width, feat_half).ast...  74.5 us
    reduce_scatter x1, waiting for transfers between devices, shards(): lax.psum_scatter(back_partial.reshape(col_blocks * width, feat_half).asty...  58 us
    scatter-add x1, other arithmetic, shards(): jnp.zeros((col_blocks, width, feat_half), jnp.float32).at[block_cols]  51.9 us
    all_gather x1, waiting for transfers between devices, shards(): spread_panel = lax.all_gather(spread, 'col', axis=0, tiled=True)  50.7 us
    all_gather x1, waiting for transfers between devices, shards(): panel = lax.all_gather(features, 'row', axis=0, tiled=True)  42.6 us
    scatter-add x1, other arithmetic, shards(): jnp.zeros((row_blocks, width, feat_half), jnp.float32).at[block_rows]  33.2 us
  transfers between devices with their start and end apart: 6, of which 6 were waited for; matrix products, arithmetic and copies ran while one was open for 7% of the time, Pallas kernels for 0%

commit v1 on v0

--- a/solution.py
+++ b/solution.py
@@ -2,6 +2,11 @@
 import jax.numpy as jnp
 from jax import lax
 from jax.sharding import PartitionSpec as P
+
+
+def by_each_axis(value, first, second):
+    half = lax.psum(value, first)
+    return lax.psum(half, second)
 
 
 def shards(features, tile_rows, tile_cols, tile_count, tile_values, weights, cotangent):
@@ -45,7 +50,7 @@
     weight_term = lax.dot_general(
         summed, grad_whole, (((0,), (0,)), ((), ())), preferred_element_type=jnp.float32
     )
-    weight_grad = lax.psum(weight_term, ("row", "col")) * node_total ** (-0.5)
+    weight_grad = by_each_axis(weight_term, "row", "col") * node_total ** (-0.5)
     spread = lax.dot_general(
         grad_whole, weight_rows, (((1,), (1,)), ((), ())), preferred_element_type=jnp.float32
     ).astype(jnp.bfloat16)

time: 1470 us -> 563 us (0.38)
  waiting for transfers between devices: 1260 us -> 354 us
    psum x1 -> x2, waiting for transfers between devices: 1020 us -> 109 us  [the longest x1 109 us: by_each_axis(): half = lax.psum(value, first)]
  transfers between devices with their start and end apart: 6 -> 7, of which waited for: 6 -> 6; matrix products, arithmetic and copies ran while one was open for 7% -> 19% of each run, Pallas kernels for 0% -> 0%
where the time goes in v1:
time: 563 us; the launch traced here: 561 us
  waiting for transfers between devices  354 us (63%)
  other arithmetic  93.8 us (17%)
  local copies, waits for them, and re-layouts  59.5 us (11%)
  matrix products  32.2 us (6%)
  between operations  14.9 us (3%)
  blocking collectives  5.89 us (1%)
    psum x1, waiting for transfers between devices, by_each_axis(): half = lax.psum(value, first)  109 us
    reduce_scatter x1, waiting for transfers between devices, shards(): lax.psum_scatter(partial_value.reshape(row_blocks * width, feat_half).ast...  74.5 us
    reduce_scatter x1, waiting for transfers between devices, shards(): lax.psum_scatter(back_partial.reshape(col_blocks * width, feat_half).asty...  57.5 us
    all_gather x1, waiting for transfers between devices, shards(): spread_panel = lax.all_gather(spread, 'col', axis=0, tiled=True)  54.1 us
    scatter-add x1, other arithmetic, shards(): jnp.zeros((col_blocks, width, feat_half), jnp.float32).at[block_cols]  51.8 us
    all_gather x1, waiting for transfers between devices, shards(): panel = lax.all_gather(features, 'row', axis=0, tiled=True)  42.6 us
    scatter-add x1, other arithmetic, shards(): jnp.zeros((row_blocks, width, feat_half), jnp.float32).at[block_rows]  33.2 us
    mul x1, local copies, waits for them, and re-layouts, shards(): back_products = back_products * live_mask[:, None, None]  17.5 us
  transfers between devices with their start and end apart: 7, of which 6 were waited for; matrix products, arithmetic and copies ran while one was open for 19% of the time, Pallas kernels for 0%

profile of v1, /device:TPU:2, one launch (start us, length us, event | category | flops | bytes accessed | tf_op | source)
XLA Modules:
  0.0 560.8 jit_solution(3845216165604454085)
XLA Ops:
  7.2 0.7 all-gather.3.cloned.1.call-update
  8.6 0.7 compare_select_fusion
  9.3 0.7 compare_select_fusion.1
  10.0 42.6 %all-gather.3.cloned.1.call-done = bf16[8192,128]{1,0:T(8,128)(2,1)} async-done(((bf16[512,128]{1,0:T(8,128)(2,1)}), bf16[8192,128]{1,0:T(8,128)(2,1)}) %all-gather.3.cloned.1.call-update) | async-done | bytes 2097168 | tf_op jit(solution)/shard_map/all_gather | solution.py:27
  52.6 10.2 %gather_fusion = bf16[256,128,128]{2,1,0:T(8,128)(2,1)} fusion(bf16[64,128,128]{2,1,0:T(8,128)(2,1)} %bitcast.30, s32[1024]{0:T(1024)S(1)} %pad_clamp_fusion.1), kind=kCustom, calls=%fused_computation | custom fusion | bytes 16778240 | tf_op jit(solution)/shard_map/gather | solution.py:28
  62.8 13.0 %multiply_bitcast_fusion.1 = f32[256,128,128]{1,2,0:T(8,128)} fusion(bf16[256,128,128]{2,1,0:T(8,128)(2,1)} %gather_fusion, bf16[1,1,256,128,128]{4,3,2,1,0:T(8,128)(2,1)} %param.11, f32[256]{0:T(256)S(1)} %compare_convert_fusion), kind=kOutput, calls=%fused_computation.5 | convolution fusion | flops 1077936128 | bytes 33555456 | tf_op jit(solution)/shard_map/tij,tjf->tif/dot_general | solution.py:29
  75.8 17.5 %copy.17 = f32[256,128,128]{2,1,0:T(8,128)} copy(f32[256,128,128]{1,2,0:T(8,128)} %multiply_bitcast_fusion.1) | data formatting | bytes 33554432 | tf_op jit(solution)/shard_map/mul | solution.py:30
  93.2 0.2 broadcast_in_dim.8
  93.5 33.2 %scatter_fusion = f32[32,128,128]{2,1,0:T(8,128)S(1)} fusion(f32[32,128,128]{2,1,0:T(8,128)S(1)} %broadcast_in_dim.8, s32[256]{0:T(256)S(1)} %bitcast.37, f32[256,128,128]{2,1,0:T(8,128)} %copy.17), kind=kCustom, calls=%fused_computation.2 | custom fusion | flops 4194304 | bytes 50332672 | tf_op jit(solution)/shard_map/scatter-add | solution.py:32
  126.6 1.1 convert_element_type.38
  127.9 74.5 %reduce-scatter.6.cloned.1.call-done = bf16[512,128]{1,0:T(8,128)(2,1)} async-done(((bf16[4096,128]{1,0:T(8,128)(2,1)}), bf16[512,128]{1,0:T(8,128)(2,1)}) %reduce-scatter.6.cloned.1.call-update) | async-done | bytes 131088 | tf_op jit(solution)/shard_map/reduce_scatter | solution.py:34
  202.3 1.1 convolution_convert_fusion
  203.5 0.8 copy.22
  204.3 0.0 all-reduce.3.cloned.1.call-start
  204.4 16.0 %reduce-scatter.10.cloned.1.call-done = bf16[128,512]{1,0:T(8,128)(2,1)} async-done(((bf16[256,512]{1,0:T(8,128)(2,1)}), bf16[128,512]{1,0:T(8,128)(2,1)}) %reduce-scatter.10.cloned.1.call-update) | async-done | bytes 131088
  220.4 1.0 copy.23
  221.4 0.8 fusion.6
  222.2 5.9 %all_gather.10 = bf16[512,256]{1,0:T(8,128)(2,1)S(1)} all-gather(bf16[512,128]{1,0:T(8,128)(2,1)S(1)} %get-tuple-element.3), channel_id=1, replica_groups=mesh['row'=16,'col'=8,'feat'=2] {'feat'}, dimensions={1}, use_global_device_ids=true | all-gather | bytes 393216 | tf_op jit(solution)/shard_map/all_gather | solution.py:49
  228.1 1.8 fusion.12
  230.0 0.9 convolution_convert_fusion.1
  230.9 0.0 all-reduce.5.cloned.1.call-start
  231.0 108.6 %all-reduce.3.cloned.1.call-done = f32[128,256]{1,0:T(8,128)} async-done(((f32[128,256]{1,0:T(8,128)}), f32[128,256]{1,0:T(8,128)}) %all-reduce.3.cloned.1.call-update) | async-done | bytes 131088 | tf_op jit(solution)/shard_map/psum | solution.py:8
  339.6 0.2 reduce-scatter.8.cloned.1.call-start
  339.9 54.1 %all-gather.5.cloned.1.call-done = bf16[4096,128]{1,0:T(8,128)(2,1)} async-done(((bf16[512,128]{1,0:T(8,128)(2,1)}), bf16[4096,128]{1,0:T(8,128)(2,1)}) %all-gather.5.cloned.1.call-update) | async-done | bytes 1048592 | tf_op jit(solution)/shard_map/all_gather | solution.py:57
  394.0 9.8 %gather_fusion.1 = bf16[256,128,128]{2,1,0:T(8,128)(2,1)} fusion(bf16[32,128,128]{2,1,0:T(8,128)(2,1)} %bitcast.29, s32[1024]{0:T(1024)S(1)} %pad_clamp_fusion), kind=kCustom, calls=%fused_computation.1 | custom fusion | bytes 16778240 | tf_op jit(solution)/shard_map/gather | solution.py:58
  403.8 15.4 %multiply_bitcast_fusion = f32[256,128,128]{1,2,0:T(8,128)} fusion(bf16[256,128,128]{2,1,0:T(8,128)(2,1)} %gather_fusion.1, bf16[1,1,256,128,128]{4,3,2,1,0:T(8,128)(2,1)} %param.11, f32[256]{0:T(256)S(1)} %compare_convert_fusion), kind=kOutput, calls=%fused_computation.4 | convolution fusion | flops 1077936128 | bytes 33555456 | tf_op jit(solution)/shard_map/tji,tjf->tif/dot_general | solution.py:59
  419.2 17.5 %copy.19 = f32[256,128,128]{2,1,0:T(8,128)} copy(f32[256,128,128]{1,2,0:T(8,128)} %multiply_bitcast_fusion) | data formatting | bytes 33554432 | tf_op jit(solution)/shard_map/mul | solution.py:62
  436.7 2.4 broadcast_in_dim.9
  439.1 51.8 %scatter_fusion.1 = f32[64,128,128]{2,1,0:T(8,128)} fusion(f32[64,128,128]{2,1,0:T(8,128)} %broadcast_in_dim.9, s32[256]{0:T(256)S(1)} %bitcast.36, f32[256,128,128]{2,1,0:T(8,128)} %copy.19), kind=kCustom, calls=%fused_computation.3 | custom fusion | flops 4194304 | bytes 50332672 | tf_op jit(solution)/shard_map/scatter-add | solution.py:64
  491.0 3.9 convert_element_type.46
  494.9 1.6 broadcast_multiply_fusion
  496.5 57.5 %reduce-scatter.8.cloned.1.call-done = bf16[512,128]{1,0:T(8,128)(2,1)} async-done(((bf16[8192,128]{1,0:T(8,128)(2,1)}), bf16[512,128]{1,0:T(8,128)(2,1)}) %reduce-scatter.8.cloned.1.call-update) | async-done | bytes 131088 | tf_op jit(solution)/shard_map/reduce_scatter | solution.py:66
  (20 shorter events, 0.3 us)
Async XLA Ops:
  7.2 195.2 %copy-start = (bf16[256,256]{1,0:T(8,128)(2,1)S(1)}, bf16[256,256]{1,0:T(8,128)(2,1)}, u32[]{:S(2)}) copy-start(bf16[256,256]{1,0:T(8,128)(2,1)} %param.12) | copy-start | bytes 393220
  7.2 45.4 %all-gather.3.cloned.1.call-start = ((), (), s32[]{:S(2)}) async-start(), calls=%async_computation.3 | async-start | bytes 2228224 | tf_op jit(solution)/shard_map/all_gather | solution.py:27
  7.9 194.4 %reduce-scatter.6.cloned.1.call-start = ((), (), s32[]{:S(2)}) async-start(), calls=%async_computation.4 | async-start | bytes 1179648 | tf_op jit(solution)/shard_map/reduce_scatter | solution.py:34
  93.4 128.0 %copy-start.2 = (bf16[512,128]{1,0:T(8,128)(2,1)S(1)}, bf16[512,128]{1,0:T(8,128)(2,1)}, u32[]{:S(2)}) copy-start(bf16[512,128]{1,0:T(8,128)(2,1)} %param.13) | copy-start | bytes 393220
  127.8 92.6 %reduce-scatter.10.cloned.1.call-start = ((), (), s32[]{:S(2)}) async-start(), calls=%async_computation.9 | async-start | bytes 393216
  204.3 135.3 %all-reduce.3.cloned.1.call-start = ((), (), s32[]{:S(2)}) async-start(), calls=%async_computation.7 | async-start | bytes 262144 | tf_op jit(solution)/shard_map/psum | solution.py:8
  229.9 164.1 %all-gather.5.cloned.1.call-start = ((), (), s32[]{:S(2)}) async-start(), calls=%async_computation.5 | async-start | bytes 1179648 | tf_op jit(solution)/shard_map/all_gather | solution.py:57
  230.9 264.0 %all-reduce.5.cloned.1.call-start = ((), (), s32[]{:S(2)}) async-start(), calls=%async_computation.8 | async-start | bytes 262144 | tf_op jit(solution)/shard_map/psum | solution.py:9
  339.6 214.3 %reduce-scatter.8.cloned.1.call-start = ((), (), s32[]{:S(2)}) async-start(), calls=%async_computation.6 | async-start | bytes 2228224 | tf_op jit(solution)/shard_map/reduce_scatter | solution.py:66
  439.1 114.8 %copy-start.1 = (bf16[256,256]{1,0:T(8,128)(2,1)S(1)}, bf16[256,256]{1,0:T(8,128)(2,1)}, u32[]{:S(2)}) copy-start(bf16[256,256]{1,0:T(8,128)(2,1)} %param.12) | copy-start | bytes 393220
Sparse Core Ops, SparseCore 0:
  9.8 42.6 all-gather.2
  127.9 74.3 reduce-scatter.5
  205.0 15.3 reduce-scatter.9
  230.1 109.5 all-reduce.2
  343.0 50.9 all-gather.4
  396.6 87.8 all-reduce.4
  495.0 58.8 reduce-scatter.7
